TPU v7x, 32 devices: a whole 2x2x4 slice. The times are simulated.
32 devices in a mesh: ctx: 8 (over y, x, core), head: 4 (over z).
Axes of the slice: x: 2, y: 2, z: 4, core: 2. Of those that a mesh axis runs over, the one named last changes fastest.
Arguments:
- block_order: int32 [16], replicated, may hold values from 0 to 15, as said below
- query_latent: bfloat16 [1024, 128, 576], P('ctx', 'head'), may hold values from -12 to 12
- key_latent: bfloat16 [1024, 576], P('ctx'), may hold values from -6 to 6
- normalizer: float32 [1024, 128], P('ctx', 'head'), may hold values from 6 to 9
- indexer_query: bfloat16 [1024, 64, 128], P('ctx', 'head'), may hold values from -8 to 8
- indexer_key: bfloat16 [1024, 128], P('ctx'), may hold values from -4 to 4
- indexer_weight: bfloat16 [1024, 64], P('ctx', 'head'), may hold values from -4 to 4
Outputs:
- query_grad: float32 [1024, 64, 128], P('ctx', 'head')
- key_grad: float32 [1024, 128], P(('ctx', 'head'))
Inputs may be any that keep to these rules, and one draw needn't show every extreme that they name: `block_order`: entries 2 i and 2 i + 1 are the blocks stored on ctx index i; all entries together are each of 0 to 15 once, and the two entries of one index sum to 15.
All inputs are finite; a program needn't handle non-finite values.
Results may differ from a plain program's by a relative error of at most 0.0037.
Values may be sent and summed in bfloat16 or wider, within the bound.
A program may use at most 128 MiB of HBM per device.

v0:
```python
import functools
import math

import jax
import jax.numpy as jnp
from jax import lax
from jax.experimental import pallas as pl
from jax.experimental.pallas import tpu as pltpu
from jax.sharding import PartitionSpec as P

MESH = pl.DeviceIdType.MESH
mla_scale = 192.0 ** (-0.5)
loss_scale = 64.0
log2e = math.log2(math.e)
NT_DIMS = (((1,), (1,)), ((), ()))
TN_DIMS = (((0,), (0,)), ((), ()))


def enter(groups, shares):
    ctx, head = lax.axis_index("ctx"), lax.axis_index("head")
    group, core = ctx // 2, lax.rem(ctx, 2)
    barrier = pltpu.get_barrier_semaphore()
    count = 0
    if groups:
        for step in range(1, groups):
            peer = lax.rem(group + step, groups) * 2 + core
            pl.semaphore_signal(barrier, 1, device_id={"ctx": peer}, device_id_type=MESH)
        pl.semaphore_signal(
            barrier, 1, device_id={"ctx": group * 2 + 1 - core}, device_id_type=MESH
        )
        count += groups
    for step in range(1, shares):
        peer = lax.rem(head + step, shares)
        pl.semaphore_signal(barrier, 1, device_id={"head": peer}, device_id_type=MESH)
    count += shares - 1
    pl.semaphore_wait(barrier, count)


def remote(src, dst, send, recv, device):
    return pltpu.make_async_remote_copy(
        src_ref=src, dst_ref=dst, send_sem=send, recv_sem=recv, device_id=device, device_id_type=MESH
    )


def partner(group, step, groups):
    bit = 1
    while bit < groups:
        if step & bit:
            group = group + bit * (1 - 2 * lax.rem(group // bit, 2))
        bit *= 2
    return group


def gather_kernel(
    groups, shares, lat, idx, iq, iw, q_far, norm, acc, all_idx, iq_recv, iw_recv,
    all_lat, q, keys, local, qs, qr, ws, wr, ds, dr, fs, fr,
):
    ctx, head = lax.axis_index("ctx"), lax.axis_index("head")
    group, core = ctx // 2, lax.rem(ctx, 2)
    sibling = group * 2 + 1 - core
    rows = idx.shape[0]
    half = rows // 2
    share = half // shares
    own = [
        pltpu.make_async_copy(lat, all_lat.at[ctx], local.at[0]),
        pltpu.make_async_copy(idx, all_idx.at[ctx], local.at[1]),
    ]
    for e in range(2):
        take = pl.ds(pl.multiple_of(e * half + head * share, share), share)
        own.append(pltpu.make_async_copy(iq.at[take], iq_recv.at[head, e], local.at[2 + e]))
    own.append(pltpu.make_async_copy(iw, iw_recv.at[head], local.at[4]))
    own.append(pltpu.make_async_copy(q_far, q, local.at[5]))
    for copy in own:
        copy.start()
    heads, bundle = q.shape[0], 8

    def score(source):
        keys[...] = jnp.concatenate((all_lat[2 * source], all_lat[2 * source + 1]), axis=1).T

        def body(i, total):
            shift = norm[pl.ds(pl.multiple_of(i * bundle, bundle), bundle), :] * log2e
            for h in range(0, bundle, 2):
                pair = jnp.concatenate((q[i * bundle + h], q[i * bundle + h + 1]), axis=1)
                scores = jnp.dot(keys[...], pair, preferred_element_type=jnp.float32) * (
                    mla_scale * log2e
                )
                total = total + jnp.exp2(scores[:, :rows] - shift[h : h + 1])
                total = total + jnp.exp2(scores[:, rows:] - shift[h + 1 : h + 2])
            return total

        acc[source] = lax.fori_loop(
            0, heads // bundle, body, jnp.zeros((2 * rows, rows), jnp.float32)
        )

    enter(groups, shares)
    sent = []
    for step in range(1, groups):
        peer = partner(group, step, groups) * 2 + core
        for k, (src, dst) in enumerate(((lat, all_lat), (idx, all_idx))):
            copy = remote(src, dst.at[ctx], ds.at[k, step], dr.at[k, step], {"ctx": peer})
            copy.start()
            sent.append(copy)
    for k, (src, dst) in enumerate(((lat, all_lat), (idx, all_idx))):
        copy = remote(src, dst.at[ctx], fs.at[k, 0], fr.at[k, 0], {"ctx": sibling})
        copy.start()
        sent.append(copy)
    for step in range(1, shares):
        peer = lax.rem(head + step, shares)
        for e in range(2):
            take = pl.ds(pl.multiple_of(e * half + peer * share, share), share)
            copy = remote(
                iq.at[take], iq_recv.at[head, e], qs.at[step, e], qr.at[step, e], {"head": peer}
            )
            copy.start()
            sent.append(copy)
        copy = remote(iw, iw_recv.at[head], ws.at[step], wr.at[step], {"head": peer})
        copy.start()
        sent.append(copy)
    slot = all_lat.at[sibling]
    remote(slot, slot, fs.at[0, 0], fr.at[0, 0], {"ctx": sibling}).wait_recv()
    own[0].wait()
    own[-1].wait()
    score(group)
    slot = all_idx.at[sibling]
    remote(slot, slot, fs.at[1, 0], fr.at[1, 0], {"ctx": sibling}).wait_recv()

    def relay(step):
        source = partner(group, step, groups) * 2 + core
        for k, dst in enumerate((all_lat, all_idx)):
            slot = dst.at[source]
            remote(slot, slot, ds.at[k, step], dr.at[k, step], {"ctx": sibling}).wait_recv()
            copy = remote(slot, slot, fs.at[k, step], fr.at[k, step], {"ctx": sibling})
            copy.start()
            sent.append(copy)

    def consume(step):
        source = partner(group, step, groups)
        for k, dst in enumerate((all_lat, all_idx)):
            slot = dst.at[source * 2 + 1 - core]
            remote(slot, slot, fs.at[k, step], fr.at[k, step], {"ctx": sibling}).wait_recv()
        score(source)

    for step in range(1, groups + 1):
        if step < groups:
            relay(step)
        if 0 < step - 1 < groups:
            consume(step - 1)
    for step in range(1, shares):
        source = lax.rem(head + shares - step, shares)
        for e in range(2):
            slot = iq_recv.at[source, e]
            remote(slot, slot, qs.at[step, e], qr.at[step, e], {"head": source}).wait_recv()
        slot = iw_recv.at[source]
        remote(slot, slot, ws.at[step], wr.at[step], {"head": source}).wait_recv()
    for copy in sent:
        copy.wait_send()
    for copy in own[1:-1]:
        copy.wait()


def gather(lat, idx, iq, iw, q, norm, cycle, shares):
    groups = cycle // 2
    rows = idx.shape[0]
    share = rows // 2 // shares
    dma = pltpu.SemaphoreType.DMA
    return pl.pallas_call(
        functools.partial(gather_kernel, groups, shares),
        out_shape=(
            jax.ShapeDtypeStruct((groups, 2 * rows, rows), jnp.float32),
            jax.ShapeDtypeStruct((cycle,) + idx.shape, idx.dtype),
            jax.ShapeDtypeStruct((shares, 2, share) + iq.shape[1:], iq.dtype),
            jax.ShapeDtypeStruct((shares,) + iw.shape, iw.dtype),
        ),
        in_specs=[pl.BlockSpec(memory_space=pl.ANY)] * 5
        + [pl.BlockSpec(memory_space=pltpu.VMEM)],
        out_specs=[pl.BlockSpec(memory_space=pltpu.VMEM)] * 4,
        scratch_shapes=[
            pltpu.VMEM((cycle,) + lat.shape, lat.dtype),
            pltpu.VMEM(q.shape, q.dtype),
            pltpu.VMEM((2 * rows, lat.shape[0]), lat.dtype),
            dma((6,)),
            dma((shares, 2)), dma((shares, 2)), dma((shares,)), dma((shares,)),
            dma((2, groups)), dma((2, groups)), dma((2, groups)), dma((2, groups)),
        ],
        compiler_params=pltpu.CompilerParams(collective_id=0, has_side_effects=True),
        name="gather",
    )(lat, idx, iq, iw, q, norm)


def forward_kernel(
    shares, tile, order, lat, idx, iq, iw, sums, probs, idx_sorted, logits, acc
):
    ctx, head = lax.axis_index("ctx"), lax.axis_index("head")
    blocks = order.shape[0]
    tokens = idx.shape[0]
    half = tokens // blocks
    rows = 2 * half
    tiles = tokens // tile
    share = half // shares
    idx_heads = iq.shape[3]
    idx_scale = (idx_heads * shares * iq.shape[4]) ** (-0.5)

    def sort(c, carry):
        for e in range(2):
            src = pl.ds(pl.multiple_of((2 * c + e) * half, half), half)
            dst = pl.ds(pl.multiple_of(order[2 * c + e] * half, half), half)
            acc[dst, :] = lat[src, :]
            idx_sorted[dst, :] = idx[src, :]
        return carry

    lax.fori_loop(0, blocks // 2, sort, 0)
    for e in range(2):
        block = order[2 * ctx + e]
        slot = (block >= blocks // 2).astype(jnp.int32)
        first = block * half + head * share
        logits[...] = jnp.full(logits.shape, -jnp.inf, jnp.float32)
        weights = []
        for z in range(shares):
            flat = iw[z].astype(jnp.float32).T * idx_scale
            flat = sum(
                jnp.where(head == y, flat[e * half + y * share : e * half + (y + 1) * share], 0.0)
                for y in range(shares)
            )
            weights.append(jnp.broadcast_to(flat[:, :, None], (share, idx_heads, 128)))

        def logit_tile(k, carry):
            cols = pl.ds(pl.multiple_of(k * tile, tile), tile)
            keys = idx_sorted[cols, :]
            total = jnp.zeros((share, tile), jnp.float32)
            for z in range(shares):
                dots = lax.dot_general(
                    iq[z, e].reshape(share * idx_heads, -1), keys, NT_DIMS,
                    preferred_element_type=jnp.float32,
                ).reshape(share, idx_heads, tile)
                parts = [
                    jnp.sum(weights[z] * jnp.maximum(dots[:, :, c : c + 128], 0.0), axis=1)
                    for c in range(0, tile, 128)
                ]
                total = total + jnp.concatenate(parts, axis=1)
            shape = (share, tile)
            visible = k * tile + lax.broadcasted_iota(
                jnp.int32, shape, 1
            ) <= first + lax.broadcasted_iota(jnp.int32, shape, 0)
            logits[:, cols] = jnp.where(visible, total, -jnp.inf)
            return carry

        lax.fori_loop(0, (block * half + half - 1) // tile + 1, logit_tile, 0)
        values = logits[...]
        top = jnp.max(values, axis=1, keepdims=True)
        expo = jnp.exp(values - top)
        norm_sum = jnp.sum(expo, axis=1, keepdims=True)
        probs[pl.ds(pl.multiple_of(slot * share, share), share), :] = expo / norm_sum

    def finish(k, carry):
        cols = pl.ds(pl.multiple_of(k * tile, tile), tile)
        total = acc[cols, :].T
        shape = (half, tile)
        for e in range(2):
            block = order[2 * ctx + e]
            slot = (block >= blocks // 2).astype(jnp.int32)
            visible = k * tile + lax.broadcasted_iota(
                jnp.int32, shape, 1
            ) <= block * half + lax.broadcasted_iota(jnp.int32, shape, 0)
            sums[pl.ds(pl.multiple_of(slot * half, half), half), cols] = jnp.where(
                visible, total[e * half : (e + 1) * half], 0.0
            )
        return carry

    lax.fori_loop(0, tiles, finish, 0)


def forward(order, lat, idx, iq, iw, shares):
    tokens, rows = lat.shape
    share = rows // 2 // shares
    vmem = pl.BlockSpec(memory_space=pltpu.VMEM)
    return pl.pallas_call(
        functools.partial(forward_kernel, shares, math.gcd(tokens // 2, 512)),
        out_shape=(
            jax.ShapeDtypeStruct((rows, tokens), jnp.float32),
            jax.ShapeDtypeStruct((2 * share, tokens), jnp.float32),
            jax.ShapeDtypeStruct(idx.shape, idx.dtype),
        ),
        in_specs=[pl.BlockSpec(memory_space=pltpu.SMEM)] + [vmem] * 4,
        out_specs=[vmem] * 3,
        scratch_shapes=[
            pltpu.VMEM((share, tokens), jnp.float32),
            pltpu.VMEM((tokens, rows), jnp.float32),
        ],
        name="forward",
    )(order, lat, idx, iq, iw)


def gradient_kernel(shares, sums, probs, grad, short_sums, low, high, ls, lr, hs, hr, gs, gr):
    head = lax.axis_index("head")
    rows, tokens = sums.shape
    half = rows // 2
    share = half // shares
    short = tokens // 2
    short_sums[...] = sums[...].astype(jnp.bfloat16)
    enter(0, shares)
    sent = []
    for step in range(1, shares):
        peer = lax.rem(head + step, shares)
        start = pl.multiple_of(peer * share, share)
        for copy in (
            remote(
                short_sums.at[pl.ds(start, share), pl.ds(0, short)], low.at[step], ls.at[step],
                lr.at[step], {"head": peer},
            ),
            remote(
                short_sums.at[pl.ds(half + start, share)], high.at[step], hs.at[step], hr.at[step],
                {"head": peer},
            ),
        ):
            copy.start()
            sent.append(copy)
    start = pl.multiple_of(head * share, share)
    total_low = sums[pl.ds(start, share), :short]
    total_high = sums[pl.ds(half + start, share), :]
    for step in range(1, shares):
        source = lax.rem(head + shares - step, shares)
        remote(low.at[step], low.at[step], ls.at[step], lr.at[step], {"head": source}).wait_recv()
        total_low = total_low + low[step].astype(jnp.float32)
        remote(high.at[step], high.at[step], hs.at[step], hr.at[step], {"head": source}).wait_recv()
        total_high = total_high + high[step].astype(jnp.float32)
    row_low = jnp.sum(total_low, axis=1, keepdims=True)
    row_high = jnp.sum(total_high, axis=1, keepdims=True)
    grad[head, 0, :, :short] = (
        loss_scale * (probs[:share, :short] - total_low / row_low)
    ).astype(jnp.bfloat16)
    grad[head, 1] = (loss_scale * (probs[share:, :] - total_high / row_high)).astype(jnp.bfloat16)
    for step in range(1, shares):
        peer = lax.rem(head + step, shares)
        for copy in (
            remote(
                grad.at[head, 0, :, pl.ds(0, short)], grad.at[head, 0, :, pl.ds(0, short)],
                gs.at[0, step], gr.at[0, step], {"head": peer},
            ),
            remote(
                grad.at[head, 1], grad.at[head, 1], gs.at[1, step], gr.at[1, step], {"head": peer}
            ),
        ):
            copy.start()
            sent.append(copy)
    for step in range(1, shares):
        source = lax.rem(head + shares - step, shares)
        slot = grad.at[source, 0, :, pl.ds(0, short)]
        remote(slot, slot, gs.at[0, step], gr.at[0, step], {"head": source}).wait_recv()
        slot = grad.at[source, 1]
        remote(slot, slot, gs.at[1, step], gr.at[1, step], {"head": source}).wait_recv()
    for copy in sent:
        copy.wait_send()


def gradient(sums, probs, shares):
    rows, tokens = sums.shape
    share = rows // 2 // shares
    dma = pltpu.SemaphoreType.DMA
    return pl.pallas_call(
        functools.partial(gradient_kernel, shares),
        out_shape=jax.ShapeDtypeStruct((shares, 2, share, tokens), jnp.bfloat16),
        in_specs=[pl.BlockSpec(memory_space=pltpu.VMEM)] * 2,
        out_specs=pl.BlockSpec(memory_space=pltpu.VMEM),
        scratch_shapes=[
            pltpu.VMEM(sums.shape, jnp.bfloat16),
            pltpu.VMEM((shares, share, tokens // 2), jnp.bfloat16),
            pltpu.VMEM((shares, share, tokens), jnp.bfloat16),
            dma((shares,)), dma((shares,)), dma((shares,)), dma((shares,)),
            dma((2, shares)), dma((2, shares)),
        ],
        compiler_params=pltpu.CompilerParams(collective_id=1, has_side_effects=True),
        name="gradient",
    )(sums, probs)


def backward_kernel(shares, tile, order, iq, iw, grad, idx, query_grad, key_grad, total, scaled):
    step, steps = pl.program_id(0), pl.num_programs(0)
    ctx = lax.axis_index("ctx")
    blocks = order.shape[0]
    tokens = idx.shape[0]
    half = tokens // blocks
    count, heads, dim = iq.shape
    share = grad.shape[2]
    parts_each = count // share
    idx_scale = (heads * shares * dim) ** (-0.5)

    @pl.when(step == 0)
    def _():
        total[...] = jnp.zeros_like(total)
        scaled[...] = iw[...].astype(jnp.float32).T * idx_scale

    e = step // (steps // 2)
    part = pl.ds(lax.rem(step, steps // 2) * parts_each, parts_each)
    block = order[2 * ctx + e]
    slot = (block >= blocks // 2).astype(jnp.int32)
    queries = iq[...].reshape(count * heads, dim)
    weights = jnp.broadcast_to(
        scaled[pl.ds(pl.multiple_of(step * count, count), count), :][:, :, None], (count, heads, 128)
    )
    query_grad[...] = jnp.zeros_like(query_grad)

    def grad_tile(k, carry):
        cols = pl.ds(pl.multiple_of(k * tile, tile), tile)
        keys = idx[cols, :]
        dots = lax.dot_general(
            queries, keys, NT_DIMS, preferred_element_type=jnp.float32
        ).reshape(count, heads, tile)
        rate = grad[part, slot, :, cols].reshape(count, tile).astype(jnp.float32)
        parts = [
            jnp.where(
                dots[:, :, c : c + 128] > 0, rate[:, None, c : c + 128] * weights, 0.0
            )
            for c in range(0, tile, 128)
        ]
        coefficient = (
            jnp.concatenate(parts, axis=2).reshape(count * heads, tile).astype(jnp.bfloat16)
        )
        query_grad[...] += jnp.dot(
            coefficient, keys, preferred_element_type=jnp.float32
        ).reshape(count, heads, dim)
        total[cols, :] += lax.dot_general(
            coefficient, queries, TN_DIMS, preferred_element_type=jnp.float32
        )
        return carry

    lax.fori_loop(0, (block * half + half - 1) // tile + 1, grad_tile, 0)

    @pl.when(step == steps - 1)
    def _():
        def store(r, carry):
            dst = pl.ds(pl.multiple_of(r * half, half), half)
            src = pl.ds(pl.multiple_of(order[r] * half, half), half)
            key_grad[dst, :] = total[src, :]
            return carry

        lax.fori_loop(0, blocks, store, 0)


def backward(order, iq, iw, grad, idx, shares):
    rows, heads, dim = iq.shape
    share = rows // 2 // shares
    count = share * shares
    tile = math.gcd(idx.shape[0] // 2, 512)
    return pl.pallas_call(
        functools.partial(backward_kernel, shares, tile),
        out_shape=(
            jax.ShapeDtypeStruct(iq.shape, jnp.float32),
            jax.ShapeDtypeStruct(idx.shape, jnp.float32),
        ),
        grid_spec=pltpu.PrefetchScalarGridSpec(
            num_scalar_prefetch=1,
            grid=(rows // count,),
            in_specs=[
                pl.BlockSpec((count, heads, dim), lambda i, o: (i, 0, 0)),
                pl.BlockSpec(iw.shape, lambda i, o: (0, 0)),
                pl.BlockSpec(grad.shape, lambda i, o: (0, 0, 0, 0)),
                pl.BlockSpec(idx.shape, lambda i, o: (0, 0)),
            ],
            out_specs=[
                pl.BlockSpec((count, heads, dim), lambda i, o: (i, 0, 0)),
                pl.BlockSpec(idx.shape, lambda i, o: (0, 0)),
            ],
            scratch_shapes=[
                pltpu.VMEM(idx.shape, jnp.float32), pltpu.VMEM((rows, heads), jnp.float32)
            ],
        ),
        name="backward",
    )(order, iq, iw, grad, idx)


def reduce_kernel(groups, shares, parts, out, near, mid, far, acc, last, ns, nr, ms, mr, fs, fr):
    ctx, head = lax.axis_index("ctx"), lax.axis_index("head")
    group, core = ctx // 2, lax.rem(ctx, 2)
    sibling = group * 2 + 1 - core
    rows = out.shape[0]
    enter(groups, shares)
    sent = []
    for step in [*range(1, groups), 0]:
        peer = lax.rem(group + step, groups)
        copy = remote(
            parts.at[peer * 2 + 1 - core], near.at[step], ns.at[step], nr.at[step], {"ctx": sibling}
        )
        copy.start()
        sent.append(copy)
    for step in range(1, groups):
        peer = lax.rem(group + step, groups)
        remote(near.at[step], near.at[step], ns.at[step], nr.at[step], {"ctx": sibling}).wait_recv()
        acc[step] = (parts[peer * 2 + core] + near[step]).astype(jnp.bfloat16)
        copy = remote(
            acc.at[step], mid.at[step], ms.at[step], mr.at[step], {"ctx": peer * 2 + core}
        )
        copy.start()
        sent.append(copy)
    remote(near.at[0], near.at[0], ns.at[0], nr.at[0], {"ctx": sibling}).wait_recv()
    value = parts[ctx] + near[0]
    for step in range(1, groups):
        remote(mid.at[step], mid.at[step], ms.at[step], mr.at[step], {"ctx": sibling}).wait_recv()
        value = value + mid[step].astype(jnp.float32)
    last[...] = value
    for step in range(1, shares):
        peer = lax.rem(head + step, shares)
        copy = remote(
            last.at[pl.ds(pl.multiple_of(peer * rows, rows), rows)], far.at[step], fs.at[step],
            fr.at[step], {"head": peer},
        )
        copy.start()
        sent.append(copy)
    value = last[pl.ds(pl.multiple_of(head * rows, rows), rows), :]
    for step in range(1, shares):
        remote(far.at[step], far.at[step], fs.at[step], fr.at[step], {"head": head}).wait_recv()
        value = value + far[step]
    out[...] = value
    for copy in sent:
        copy.wait_send()


def reduce(parts, cycle, shares):
    groups = cycle // 2
    rows, dim = parts.shape[0] // cycle, parts.shape[1]
    dma = pltpu.SemaphoreType.DMA
    buffer = pltpu.VMEM((groups, rows, dim), jnp.bfloat16)
    return pl.pallas_call(
        functools.partial(reduce_kernel, groups, shares),
        out_shape=jax.ShapeDtypeStruct((rows // shares, dim), jnp.float32),
        in_specs=[pl.BlockSpec(memory_space=pltpu.VMEM)],
        out_specs=pl.BlockSpec(memory_space=pltpu.VMEM),
        scratch_shapes=[
            pltpu.VMEM((groups, rows, dim), jnp.float32), buffer,
            pltpu.VMEM((shares, rows // shares, dim), jnp.float32), buffer,
            pltpu.VMEM((rows, dim), jnp.float32),
            dma((groups,)), dma((groups,)), dma((groups,)), dma((groups,)),
            dma((shares,)), dma((shares,)),
        ],
        compiler_params=pltpu.CompilerParams(collective_id=2, has_side_effects=True),
        name="reduce",
    )(parts.reshape(cycle, rows, dim))


def per_device(
    block_order, query_latent, key_latent, normalizer, indexer_query, indexer_key, indexer_weight
):
    cycle, shares = lax.axis_size("ctx"), lax.axis_size("head")
    weight = indexer_weight.T
    partial, idx, iq, iw = gather(
        key_latent.T, indexer_key, indexer_query, weight, query_latent.transpose(1, 2, 0),
        normalizer.T, cycle, shares,
    )
    idx = idx.reshape(-1, idx.shape[2])
    sums, probs, idx_sorted = forward(
        block_order, partial.reshape(-1, partial.shape[2]), idx, iq, iw, shares
    )
    grad = gradient(sums, probs, shares)
    query_grad, key_parts = backward(
        block_order, indexer_query, weight, grad, idx_sorted, shares
    )
    return query_grad, reduce(key_parts, cycle, shares)


def solution(mesh):
    return jax.shard_map(
        per_device,
        mesh=mesh,
        in_specs=(
            P(),
            P("ctx", "head", None),
            P("ctx", None),
            P("ctx", "head"),
            P("ctx", "head", None),
            P("ctx", None),
            P("ctx", "head"),
        ),
        out_specs=(P("ctx", "head", None), P(("ctx", "head"), None)),
        check_vma=False,
    )
```

profile of v0, /device:TPU:0, one launch (start us, length us, event | category | flops | bytes accessed | tf_op | source)
XLA Modules:
  0.0 64.9 jit_solution(13099690970648811274)
XLA Ops:
  0.6 23.3 %gather.1 = (f32[4,256,128]{2,1,0:T(8,128)}, bf16[8,128,128]{2,1,0:T(8,128)(2,1)}, bf16[4,2,16,16,128]{4,3,2,1,0:T(8,128)(2,1)}, bf16[4,16,128]{2,1,0:T(8,128)(2,1)}) custom-call(bf16[576,128]{1,0:T(8,128)(2,1)} %bitcast.11, bf16[128,128]{1,0:T(8,128)(2,1)} %idx.1, bf16[128,16,128]{2,1,0:T(8,128)(2,1)} %iq.3, bf16[16,128]{1,0:T(8,128)(2,1)} %bitcast.13, ...), custom_call_target="tpu_custom_call" | custom-call | tf_op jit(solution)/shard_map/gather/pallas_call | solution.py:166
  24.0 5.1 %forward.1 = (f32[128,1024]{1,0:T(8,128)}, f32[32,1024]{1,0:T(8,128)}, bf16[1024,128]{1,0:T(8,128)(2,1)}) custom-call(s32[16]{0:T(128)} %order.3, f32[1024,128]{1,0:T(8,128)} %bitcast.8, bf16[1024,128]{1,0:T(8,128)(2,1)} %bitcast.10, bf16[4,2,16,16,128]{4,3,2,1,0:T(8,128)(2,1)} %get-tuple-element.13.iq, bf16[4,16,128]{2,1,0:T(8,128)(2,1)} %get-tuple-element.14.iw), custom_call_target="tpu_custom_call" | custom-call | tf_op jit(solution)/shard_map/forward/pallas_call | solution.py:276
  29.0 14.0 %gradient.1.grad = bf16[4,2,16,1024]{3,2,1,0:T(8,128)(2,1)} custom-call(f32[128,1024]{1,0:T(8,128)} %get-tuple-element.15.sums, f32[32,1024]{1,0:T(8,128)} %get-tuple-element.16.probs), custom_call_target="tpu_custom_call" | custom-call | tf_op jit(solution)/shard_map/gradient/pallas_call | solution.py:359
  43.1 7.2 %backward.1 = (f32[128,16,128]{2,1,0:T(8,128)}, f32[1024,128]{1,0:T(8,128)}) custom-call(s32[16]{0:T(128)} %order.3, bf16[128,16,128]{2,1,0:T(8,128)(2,1)} %iq.3, bf16[16,128]{1,0:T(8,128)(2,1)} %bitcast.14, bf16[4,2,16,1024]{3,2,1,0:T(8,128)(2,1)} %gradient.1.grad, bf16[1024,128]{1,0:T(8,128)(2,1)} %get-tuple-element.17.idx), custom_call_target="tpu_custom_call" | custom-call | tf_op jit(solution)/shard_map/backward/pallas_call | solution.py:444
  50.3 13.3 %reduce.1 = f32[32,128]{1,0:T(8,128)} custom-call(f32[8,128,128]{2,1,0:T(8,128)} %bitcast.9), custom_call_target="tpu_custom_call" | custom-call | tf_op jit(solution)/shard_map/reduce/pallas_call | solution.py:522
  63.6 1.3 %copy.10 = f32[32,128]{1,0:T(8,128)} copy(f32[32,128]{1,0:T(8,128)} %reduce.1) | data formatting | bytes 32768
where the time goes:
time: 65.2 us; the launch traced here: 64.9 us
  Pallas kernels  62.9 us (96%)
  local copies, waits for them, and re-layouts  1.32 us (2%)
  between operations  0.66 us (1%)
    pallas_call x1, Pallas kernels, gather(): pl.pallas_call(functools.partial(gather_kernel, groups, shares), out_shap...  23.3 us
    pallas_call x1, Pallas kernels, gradient(): pl.pallas_call(functools.partial(gradient_kernel, shares), out_shape=jax....  14 us
    pallas_call x1, Pallas kernels, reduce(): pl.pallas_call(functools.partial(reduce_kernel, groups, shares), out_shap...  13.3 us
    pallas_call x1, Pallas kernels, backward(): pl.pallas_call(functools.partial(backward_kernel, shares, tile), out_shap...  7.2 us
    pallas_call x1, Pallas kernels, forward(): pl.pallas_call(functools.partial(forward_kernel, shares, math.gcd(tokens...  5.06 us
    unnamed x1, local copies, waits for them, and re-layouts  1.32 us

commit v1 on v0

v1 whole, which is shorter than its diff:
```python
import functools
import math

import jax
import jax.numpy as jnp
from jax import lax
from jax.experimental import pallas as pl
from jax.experimental.pallas import tpu as pltpu
from jax.sharding import PartitionSpec as P

MESH = pl.DeviceIdType.MESH
mla_scale = 192.0 ** (-0.5)
loss_scale = 64.0
log2e = math.log2(math.e)
NT_DIMS = (((1,), (1,)), ((), ()))


def remote(src, dst, send, recv, device):
    return pltpu.make_async_remote_copy(
        src_ref=src, dst_ref=dst, send_sem=send, recv_sem=recv, device_id=device, device_id_type=MESH
    )


def partner(group, step, groups):
    bit = 1
    while bit < groups:
        if step & bit:
            group = group + bit * (1 - 2 * lax.rem(group // bit, 2))
        bit *= 2
    return group


def kernel(
    groups, shares, order, lat, idx, iq, iw_far, q_far, norm_far, qg_out, kg_out,
    all_lat, all_idx, q, iq_near, iqf, iw, norm, keys, keys_t, coefs, rate,
    lsend, tsend, lrecv, trecv, gall, ksend, krecv, kown, kz, kzr, qg,
    local, ds, dr, fs, fr, xs, xr, gs, gr, ks, kr, zs, zr,
):
    ctx, head = lax.axis_index("ctx"), lax.axis_index("head")
    group, core = ctx // 2, lax.rem(ctx, 2)
    sibling = group * 2 + 1 - core
    blocks = order.shape[0]
    rows, dim = idx.shape
    half = rows // 2
    share = half // shares
    heads, idx_heads = q.shape[0], iw.shape[0]
    bundle = 8
    idx_scale = (idx_heads * shares * dim) ** (-0.5)

    own = [
        pltpu.make_async_copy(iq, iq_near, local.at[0]),
        pltpu.make_async_copy(iw_far, iw, local.at[1]),
        pltpu.make_async_copy(idx, all_idx.at[ctx], local.at[2]),
        pltpu.make_async_copy(lat, all_lat.at[ctx], local.at[3]),
        pltpu.make_async_copy(norm_far, norm, local.at[4]),
        pltpu.make_async_copy(q_far, q, local.at[5]),
    ]
    for copy in own:
        copy.start()
    barrier = pltpu.get_barrier_semaphore()
    for step in range(1, groups):
        peer = partner(group, step, groups) * 2
        for j in range(2):
            pl.semaphore_signal(barrier, 1, device_id={"ctx": peer + j}, device_id_type=MESH)
    pl.semaphore_signal(barrier, 1, device_id={"ctx": sibling}, device_id_type=MESH)
    for step in range(1, shares):
        peer = lax.rem(head + step, shares)
        pl.semaphore_signal(barrier, 1, device_id={"head": peer}, device_id_type=MESH)
    own[0].wait()
    iqf[...] = jnp.swapaxes(iq_near[...], 0, 1).reshape(idx_heads * rows, dim)
    pl.semaphore_wait(barrier, 2 * (groups - 1) + 1 + shares - 1)

    sent = []

    def go(copy):
        copy.start()
        sent.append(copy)

    for k, (src, dst) in enumerate(((idx, all_idx), (lat, all_lat))):
        go(remote(src, dst.at[ctx], fs.at[k, 0], fr.at[k, 0], {"ctx": sibling}))
        for step in range(1, groups):
            peer = partner(group, step, groups) * 2 + core
            go(remote(src, dst.at[ctx], ds.at[k, step], dr.at[k, step], {"ctx": peer}))

    def relay(k, step):
        source = partner(group, step, groups) * 2 + core
        slot = (all_idx, all_lat)[k].at[source]
        remote(slot, slot, ds.at[k, step], dr.at[k, step], {"ctx": sibling}).wait_recv()
        go(remote(slot, slot, fs.at[k, step], fr.at[k, step], {"ctx": sibling}))

    def arrive(k, step):
        slot = (all_idx, all_lat)[k].at[partner(group, step, groups) * 2 + 1 - core]
        remote(slot, slot, fs.at[k, step], fr.at[k, step], {"ctx": sibling}).wait_recv()

    def swapped(c):
        return order[2 * c] >= blocks // 2

    def lowest(c):
        return jnp.minimum(order[2 * c], order[2 * c + 1])

    mine_swapped, mine = swapped(ctx), lowest(ctx)
    lane = lax.broadcasted_iota(jnp.int32, (half, rows), 1)

    def turn(x):
        return pltpu.roll(x, half, 1)

    def pack(total, source):
        total = total.T
        first, second = total[:half], total[half:]
        hi = jnp.where(mine_swapped, first, second)
        lo = jnp.where(mine_swapped, second, first)
        packed, low = [], []
        for j in range(2):
            c = 2 * source + j
            flip, early = swapped(c), lowest(c) < mine
            h, l = hi[:, j * rows : (j + 1) * rows], lo[:, j * rows : (j + 1) * rows]
            a = jnp.where(flip, turn(h), h)
            b = jnp.where(flip, l, turn(l))
            packed.append(jnp.where(early & (lane >= half), b, a))
            low.append(b)
        return jnp.concatenate(packed, axis=1), jnp.where(core == 0, low[0], low[1])

    def unpack(slot, source):
        piece = jnp.concatenate([gall[z, slot] for z in range(shares)], axis=0)
        piece = piece.astype(jnp.float32)
        his, los = [], []
        for j in range(2):
            c = 2 * source + j
            flip, early = swapped(c), lowest(c) < mine
            x = piece[:, j * rows : (j + 1) * rows]
            low_lanes = early & (lane >= half)
            h = jnp.where(low_lanes, 0.0, x)
            l = jnp.where(low_lanes, x, 0.0)
            if slot == 0:
                extra = jnp.concatenate(
                    [gall[z, groups, :, :rows] for z in range(shares)], axis=0
                ).astype(jnp.float32)
                l = jnp.where(core == j, extra, l)
            his.append(jnp.where(flip, turn(h), h))
            los.append(jnp.where(flip, l, turn(l)))
        hi, lo = jnp.concatenate(his, axis=1), jnp.concatenate(los, axis=1)
        first = jnp.where(mine_swapped, hi, lo)
        second = jnp.where(mine_swapped, lo, hi)
        return jnp.concatenate((first, second), axis=0).T

    def exchange(k, slot, width):
        send, recv = ((lsend, lrecv), (tsend, trecv))[k]
        for step in range(1, shares):
            peer = lax.rem(head + step, shares)
            go(
                remote(
                    send.at[peer, slot, :, pl.ds(0, width)],
                    recv.at[step, slot, :, pl.ds(0, width)],
                    xs.at[k, slot, step], xr.at[k, slot, step], {"head": peer},
                )
            )

    def deal(k, slot, packed):
        send = (lsend, tsend)[k]
        for z in range(shares):
            send[z, slot, :, : packed.shape[1]] = packed[z * share : (z + 1) * share].astype(
                send.dtype
            )
        exchange(k, slot, packed.shape[1])

    def logits(step):
        source = partner(group, step, groups)
        chip = jnp.concatenate((all_idx[2 * source], all_idx[2 * source + 1]), axis=0)
        keys_t[:, step * 2 * rows : (step + 1) * 2 * rows] = chip.T
        total = jnp.zeros((2 * rows, rows), jnp.float32)
        for p in range(idx_heads // 2):
            cols = slice(2 * p * rows, 2 * (p + 1) * rows)
            dots = lax.dot_general(
                chip, iqf[cols, :], NT_DIMS, preferred_element_type=jnp.float32
            )
            coefs[step * 2 * rows : (step + 1) * 2 * rows, cols] = jnp.where(
                dots > 0, 1.0, 0.0
            ).astype(jnp.bfloat16)
            dots = jnp.maximum(dots, 0.0)
            total = total + dots[:, :rows] * weights[2 * p : 2 * p + 1]
            total = total + dots[:, rows:] * weights[2 * p + 1 : 2 * p + 2]
        packed, low = pack(total, source)
        deal(0, step, packed)
        if step == 0:
            deal(0, groups, low)

    def score(step):
        source = partner(group, step, groups)
        keys[...] = jnp.concatenate((all_lat[2 * source], all_lat[2 * source + 1]), axis=1).T

        def body(i, total):
            shift = norm[pl.ds(pl.multiple_of(i * bundle, bundle), bundle), :] * log2e
            for h in range(0, bundle, 2):
                pair = jnp.concatenate((q[i * bundle + h], q[i * bundle + h + 1]), axis=1)
                scores = jnp.dot(keys[...], pair, preferred_element_type=jnp.float32) * (
                    mla_scale * log2e
                )
                total = total + jnp.exp2(scores[:, :rows] - shift[h : h + 1])
                total = total + jnp.exp2(scores[:, rows:] - shift[h + 1 : h + 2])
            return total

        total = lax.fori_loop(
            0, heads // bundle, body, jnp.zeros((2 * rows, rows), jnp.float32)
        )
        packed, low = pack(total, source)
        deal(1, step, packed)
        if step == 0:
            deal(1, groups, low)

    own[1].wait()
    weights = iw[...].astype(jnp.float32) * idx_scale
    own[2].wait()
    arrive_own = all_idx.at[sibling]
    remote(arrive_own, arrive_own, fs.at[0, 0], fr.at[0, 0], {"ctx": sibling}).wait_recv()
    logits(0)
    own[3].wait()
    own[4].wait()
    own[5].wait()
    arrive_own = all_lat.at[sibling]
    remote(arrive_own, arrive_own, fs.at[1, 0], fr.at[1, 0], {"ctx": sibling}).wait_recv()
    score(0)
    for step in range(1, groups):
        relay(0, step)
    for step in range(1, groups):
        arrive(0, step)
        logits(step)
        if step < 3:
            relay(1, step)
    for step in range(1, groups):
        arrive(1, step)
        score(step)
        if 2 < step + 2 < groups:
            relay(1, step + 2)

    shape = (share, 2 * rows)
    token = head * share + lax.broadcasted_iota(jnp.int32, shape, 0)
    column = lax.broadcasted_iota(jnp.int32, shape, 1)
    inner = lax.rem(column, rows)
    later = inner >= half

    def columns(slot):
        if slot == groups:
            seen = later & (inner - half <= token)
            return later[:, :rows], seen[:, :rows], rows
        source = partner(group, slot, groups)
        early = [(lowest(2 * source + j) < mine).astype(jnp.int32) for j in range(2)]
        low = later & (jnp.where(column < rows, early[0], early[1]) > 0)
        seen = None
        if slot == 0:
            mixed = (column >= core * rows) & (column < (core + 1) * rows) & later
            seen = jnp.logical_not(mixed) | (inner - half <= token)
        return low, seen, 2 * rows

    slots = [*range(groups - 1, 0, -1), 0, groups]
    table = {slot: columns(slot) for slot in slots}

    def gather_sum(k, slot):
        send, recv = ((lsend, lrecv), (tsend, trecv))[k]
        width = table[slot][2]
        value = send[head, slot, :, :width].astype(jnp.float32)
        for step in range(1, shares):
            piece = recv.at[step, slot, :, pl.ds(0, width)]
            remote(piece, piece, xs.at[k, slot, step], xr.at[k, slot, step], {"head": head}).wait_recv()
            value = value + recv[step, slot, :, :width].astype(jnp.float32)
        return value

    inf = jnp.float32(jnp.inf)

    def split(values, reduce, fill):
        his, los = [], []
        for slot, value in values.items():
            low, seen, _ = table[slot]
            h = low if seen is None else low | jnp.logical_not(seen)
            l = jnp.logical_not(low) if seen is None else jnp.logical_not(low & seen)
            his.append(reduce(jnp.where(h, fill, value), axis=1, keepdims=True))
            los.append(reduce(jnp.where(l, fill, value), axis=1, keepdims=True))
        return his, los

    scored = {slot: gather_sum(0, slot) for slot in slots}
    his, los = split(scored, jnp.max, -inf)
    hi_top, lo_top = functools.reduce(jnp.maximum, his), functools.reduce(jnp.maximum, los)
    scored = {
        slot: jnp.exp(value - jnp.where(table[slot][0], lo_top, hi_top))
        for slot, value in scored.items()
    }
    his, los = split(scored, jnp.sum, 0.0)
    hi_norm, lo_norm = loss_scale / sum(his), loss_scale / sum(los)
    target = {slot: gather_sum(1, slot) for slot in slots}
    his, los = split(target, jnp.sum, 0.0)
    hi_total, lo_total = loss_scale / sum(his), loss_scale / sum(los)
    for slot in slots:
        low, seen, width = table[slot]
        value = scored[slot] * jnp.where(low, lo_norm, hi_norm)
        value = value - target[slot] * jnp.where(low, lo_total, hi_total)
        if seen is not None:
            value = jnp.where(seen, value, 0.0)
        gall[head, slot, :, :width] = value.astype(jnp.bfloat16)
        for step in range(1, shares):
            peer = lax.rem(head + step, shares)
            piece = gall.at[head, slot, :, pl.ds(0, width)]
            go(remote(piece, piece, gs.at[slot, step], gr.at[slot, step], {"head": peer}))

    def granted(slot):
        for step in range(1, shares):
            source = lax.rem(head + shares - step, shares)
            piece = gall.at[source, slot, :, pl.ds(0, table[slot][2])]
            remote(piece, piece, gs.at[slot, step], gr.at[slot, step], {"head": source}).wait_recv()

    for slot in [*range(groups - 1, 0, -1), 0]:
        granted(slot)
        if slot == 0:
            granted(groups)
        source = partner(group, slot, groups)
        rate[...] = unpack(slot, source)
        span = slice(slot * 2 * rows, (slot + 1) * 2 * rows)
        for h in range(idx_heads):
            cols = slice(h * rows, (h + 1) * rows)
            coefs[span, cols] = (rate[...] * weights[h : h + 1]).astype(jnp.bfloat16) * coefs[
                span, cols
            ]
        total = jnp.dot(coefs[span, :], iqf[...], preferred_element_type=jnp.float32)
        if slot == 0:
            kown[...] = total.reshape(2, rows, dim)
        ksend[slot] = total.astype(jnp.bfloat16).reshape(2, rows, dim)
        if slot == 0:
            go(
                remote(
                    ksend.at[0, 1 - core], krecv.at[0, core], ks.at[0, 0], kr.at[0, core],
                    {"ctx": sibling},
                )
            )
        else:
            for j in range(2):
                go(
                    remote(
                        ksend.at[slot, j], krecv.at[slot, core], ks.at[slot, j], kr.at[slot, core],
                        {"ctx": source * 2 + j},
                    )
                )

    def query(p):
        cols = slice(2 * p * rows, 2 * (p + 1) * rows)
        value = jnp.dot(keys_t[...], coefs[:, cols], preferred_element_type=jnp.float32).T
        qg[:, 2 * p, :] = value[:rows]
        qg[:, 2 * p + 1, :] = value[rows:]

    pairs = idx_heads // 2
    for p in range(pairs // 2):
        query(p)
    value = kown[core]
    for slot in [*range(groups - 1, 0, -1), 0]:
        for k in range(2) if slot else (1 - core,):
            piece = krecv.at[slot, k]
            remote(piece, piece, ks.at[slot, 0], kr.at[slot, k], {"ctx": sibling}).wait_recv()
            value = value + krecv[slot, k].astype(jnp.float32)
    kz[...] = value
    part = rows // shares
    for step in range(1, shares):
        peer = lax.rem(head + step, shares)
        take = pl.ds(pl.multiple_of(peer * part, part), part)
        go(remote(kz.at[take], kzr.at[step], zs.at[step], zr.at[step], {"head": peer}))
    for p in range(pairs // 2, pairs):
        query(p)
    out = pltpu.make_async_copy(qg, qg_out, local.at[6])
    out.start()
    value = kz[pl.ds(pl.multiple_of(head * part, part), part), :]
    for step in range(1, shares):
        remote(kzr.at[step], kzr.at[step], zs.at[step], zr.at[step], {"head": head}).wait_recv()
        value = value + kzr[step]
    kg_out[...] = value
    for copy in sent:
        copy.wait_send()
    out.wait()


def per_device(
    block_order, query_latent, key_latent, normalizer, indexer_query, indexer_key, indexer_weight
):
    cycle, shares = lax.axis_size("ctx"), lax.axis_size("head")
    groups = cycle // 2
    rows, dim = indexer_key.shape
    heads, latent = query_latent.shape[1:]
    idx_heads = indexer_query.shape[1]
    share = rows // 2 // shares
    bf16, f32 = jnp.bfloat16, jnp.float32
    dma, vmem = pltpu.SemaphoreType.DMA, pltpu.VMEM
    return pl.pallas_call(
        functools.partial(kernel, groups, shares),
        out_shape=(
            jax.ShapeDtypeStruct((rows, idx_heads, dim), f32),
            jax.ShapeDtypeStruct((rows // shares, dim), f32),
        ),
        in_specs=[pl.BlockSpec(memory_space=pltpu.SMEM)] + [pl.BlockSpec(memory_space=pl.ANY)] * 6,
        out_specs=(pl.BlockSpec(memory_space=pl.ANY), pl.BlockSpec(memory_space=pltpu.VMEM)),
        scratch_shapes=[
            vmem((cycle, latent, rows), bf16),
            vmem((cycle, rows, dim), bf16),
            vmem((heads, latent, rows), bf16),
            vmem((rows, idx_heads, dim), bf16),
            vmem((idx_heads * rows, dim), bf16),
            vmem((idx_heads, rows), bf16),
            vmem((heads, rows), f32),
            vmem((2 * rows, latent), bf16),
            vmem((dim, cycle * rows), bf16),
            vmem((cycle * rows, idx_heads * rows), bf16),
            vmem((2 * rows, rows), f32),
            vmem((shares, groups + 1, share, 2 * rows), f32),
            vmem((shares, groups + 1, share, 2 * rows), bf16),
            vmem((shares, groups + 1, share, 2 * rows), f32),
            vmem((shares, groups + 1, share, 2 * rows), bf16),
            vmem((shares, groups + 1, share, 2 * rows), bf16),
            vmem((groups, 2, rows, dim), bf16),
            vmem((groups, 2, rows, dim), bf16),
            vmem((2, rows, dim), f32),
            vmem((rows, dim), f32),
            vmem((shares, rows // shares, dim), f32),
            vmem((rows, idx_heads, dim), f32),
            dma((7,)),
            dma((2, groups)), dma((2, groups)), dma((2, groups)), dma((2, groups)),
            dma((2, groups + 1, shares)), dma((2, groups + 1, shares)),
            dma((groups + 1, shares)), dma((groups + 1, shares)),
            dma((groups, 2)), dma((groups, 2)),
            dma((shares,)), dma((shares,)),
        ],
        compiler_params=pltpu.CompilerParams(collective_id=0, has_side_effects=True),
        name="indexer",
    )(
        block_order, key_latent.T, indexer_key, indexer_query, indexer_weight.T,
        query_latent.transpose(1, 2, 0), normalizer.T,
    )


def solution(mesh):
    return jax.shard_map(
        per_device,
        mesh=mesh,
        in_specs=(
            P(),
            P("ctx", "head", None),
            P("ctx", None),
            P("ctx", "head"),
            P("ctx", "head", None),
            P("ctx", None),
            P("ctx", "head"),
        ),
        out_specs=(P("ctx", "head", None), P(("ctx", "head"), None)),
        check_vma=False,
    )
```

time: 65.2 us -> 46.3 us (0.71)
  Pallas kernels: 62.9 us -> 41.8 us
  local copies, waits for them, and re-layouts: 1.32 us -> 3.59 us
    pallas_call x5 -> x1, Pallas kernels: 62.9 us -> 41.8 us  [per_device(): pl.pallas_call(functools.partial(kernel, groups, shares), out_shape=(jax....]
    unnamed x1 -> x2, local copies, waits for them, and re-layouts: 1.32 us -> 3.59 us
where the time goes in v1:
time: 46.3 us; the launch traced here: 46 us
  Pallas kernels  41.8 us (90%)
  local copies, waits for them, and re-layouts  3.59 us (8%)
  between operations  0.64 us (1%)
    pallas_call x1, Pallas kernels, per_device(): pl.pallas_call(functools.partial(kernel, groups, shares), out_shape=(jax....  41.8 us
    unnamed x2, local copies, waits for them, and re-layouts  3.59 us

profile of v1, /device:TPU:0, one launch (start us, length us, event | category | flops | bytes accessed | tf_op | source)
XLA Modules:
  0.0 46.0 jit_solution(15034310279968162329)
XLA Ops:
  0.6 41.8 %indexer.1 = (f32[128,16,128]{2,1,0:T(8,128)}, f32[32,128]{1,0:T(8,128)}) custom-call(s32[16]{0:T(128)} %order.1, bf16[576,128]{1,0:T(8,128)(2,1)} %bitcast.5, bf16[128,128]{1,0:T(8,128)(2,1)} %idx.1, bf16[128,16,128]{2,1,0:T(8,128)(2,1)} %iq.1, bf16[16,128]{1,0:T(8,128)(2,1)} %bitcast.7, bf16[32,576,128]{2,1,0:T(8,128)(2,1)} %bitcast.4, f32[32,128]{1,0:T(8,128)} %bitcast.6), custom_call_target="tpu_custom_call" | custom-call | tf_op jit(solution)/shard_map/indexer/pallas_call | solution.py:387
  42.5 2.3 %copy.11 = f32[128,16,128]{2,1,0:T(8,128)} copy(f32[128,16,128]{2,1,0:T(8,128)} %get-tuple-element.4) | data formatting | bytes 2097152
  44.7 1.3 %copy.12 = f32[32,128]{1,0:T(8,128)} copy(f32[32,128]{1,0:T(8,128)} %get-tuple-element.5) | data formatting | bytes 32768

commit v2 on v1

--- a/solution.py
+++ b/solution.py
@@ -31,9 +31,10 @@
 
 
 def kernel(
-    groups, shares, order, lat, idx, iq, iw_far, q_far, norm_far, qg_out, kg_out,
+    groups, shares, order_far, lat, idx, iq, iw_far, q_far, norm_far, qg, kg_out,
+    order,
     all_lat, all_idx, q, iq_near, iqf, iw, norm, keys, keys_t, coefs, rate,
-    lsend, tsend, lrecv, trecv, gall, ksend, krecv, kown, kz, kzr, qg,
+    lsend, tsend, lrecv, trecv, gall, ksend, krecv, kown, kz, kzs, kzr,
     local, ds, dr, fs, fr, xs, xr, gs, gr, ks, kr, zs, zr,
 ):
     ctx, head = lax.axis_index("ctx"), lax.axis_index("head")
@@ -54,9 +55,8 @@
         pltpu.make_async_copy(lat, all_lat.at[ctx], local.at[3]),
         pltpu.make_async_copy(norm_far, norm, local.at[4]),
         pltpu.make_async_copy(q_far, q, local.at[5]),
+        pltpu.make_async_copy(order_far, order, local.at[6]),
     ]
-    for copy in own:
-        copy.start()
     barrier = pltpu.get_barrier_semaphore()
     for step in range(1, groups):
         peer = partner(group, step, groups) * 2
@@ -66,8 +66,8 @@
     for step in range(1, shares):
         peer = lax.rem(head + step, shares)
         pl.semaphore_signal(barrier, 1, device_id={"head": peer}, device_id_type=MESH)
-    own[0].wait()
-    iqf[...] = jnp.swapaxes(iq_near[...], 0, 1).reshape(idx_heads * rows, dim)
+    for copy in own:
+        copy.start()
     pl.semaphore_wait(barrier, 2 * (groups - 1) + 1 + shares - 1)
 
     sent = []
@@ -98,6 +98,7 @@
     def lowest(c):
         return jnp.minimum(order[2 * c], order[2 * c + 1])
 
+    own[6].wait()
     mine_swapped, mine = swapped(ctx), lowest(ctx)
     lane = lax.broadcasted_iota(jnp.int32, (half, rows), 1)
 
@@ -184,52 +185,61 @@
         if step == 0:
             deal(0, groups, low)
 
+    def attend(lhs):
+        total = jnp.zeros((lhs.shape[0], rows), jnp.float32)
+        for h in range(0, heads, 2):
+            pair = jnp.concatenate((q[h], q[h + 1]), axis=1)
+            scores = jnp.dot(lhs[...], pair, preferred_element_type=jnp.float32) * (
+                mla_scale * log2e
+            )
+            shift = norm[h : h + 2, :] * log2e
+            total = total + jnp.exp2(scores[:, :rows] - shift[:1])
+            total = total + jnp.exp2(scores[:, rows:] - shift[1:])
+        return total
+
     def score(step):
         source = partner(group, step, groups)
-        keys[...] = jnp.concatenate((all_lat[2 * source], all_lat[2 * source + 1]), axis=1).T
-
-        def body(i, total):
-            shift = norm[pl.ds(pl.multiple_of(i * bundle, bundle), bundle), :] * log2e
-            for h in range(0, bundle, 2):
-                pair = jnp.concatenate((q[i * bundle + h], q[i * bundle + h + 1]), axis=1)
-                scores = jnp.dot(keys[...], pair, preferred_element_type=jnp.float32) * (
-                    mla_scale * log2e
-                )
-                total = total + jnp.exp2(scores[:, :rows] - shift[h : h + 1])
-                total = total + jnp.exp2(scores[:, rows:] - shift[h + 1 : h + 2])
-            return total
-
-        total = lax.fori_loop(
-            0, heads // bundle, body, jnp.zeros((2 * rows, rows), jnp.float32)
-        )
+        if step < groups - 1:
+            arrive(1, step)
+            keys[...] = jnp.concatenate((all_lat[2 * source], all_lat[2 * source + 1]), axis=1).T
+            total = attend(keys)
+        else:
+            parts = []
+            for k, device in enumerate((2 * source + core, 2 * source + 1 - core)):
+                if k:
+                    arrive(1, step)
+                half_keys = keys.at[pl.ds(k * rows, rows)]
+                half_keys[...] = all_lat[device].T
+                parts.append(attend(half_keys))
+            near, other = parts
+            total = jnp.concatenate(
+                (jnp.where(core == 0, near, other), jnp.where(core == 0, other, near)), axis=0
+            )
         packed, low = pack(total, source)
         deal(1, step, packed)
         if step == 0:
             deal(1, groups, low)
 
+    own[0].wait()
+    iqf[...] = jnp.swapaxes(iq_near[...], 0, 1).reshape(idx_heads * rows, dim)
     own[1].wait()
     weights = iw[...].astype(jnp.float32) * idx_scale
     own[2].wait()
-    arrive_own = all_idx.at[sibling]
-    remote(arrive_own, arrive_own, fs.at[0, 0], fr.at[0, 0], {"ctx": sibling}).wait_recv()
+    arrive(0, 0)
     logits(0)
-    own[3].wait()
-    own[4].wait()
-    own[5].wait()
-    arrive_own = all_lat.at[sibling]
-    remote(arrive_own, arrive_own, fs.at[1, 0], fr.at[1, 0], {"ctx": sibling}).wait_recv()
+    for copy in own[3:6]:
+        copy.wait()
     score(0)
     for step in range(1, groups):
         relay(0, step)
     for step in range(1, groups):
         arrive(0, step)
         logits(step)
-        if step < 3:
-            relay(1, step)
+    for step in range(1, min(3, groups)):
+        relay(1, step)
     for step in range(1, groups):
-        arrive(1, step)
         score(step)
-        if 2 < step + 2 < groups:
+        if step + 2 < groups:
             relay(1, step + 2)
 
     shape = (share, 2 * rows)
@@ -354,23 +364,21 @@
             remote(piece, piece, ks.at[slot, 0], kr.at[slot, k], {"ctx": sibling}).wait_recv()
             value = value + krecv[slot, k].astype(jnp.float32)
     kz[...] = value
+    kzs[...] = value.astype(jnp.bfloat16)
     part = rows // shares
     for step in range(1, shares):
         peer = lax.rem(head + step, shares)
         take = pl.ds(pl.multiple_of(peer * part, part), part)
-        go(remote(kz.at[take], kzr.at[step], zs.at[step], zr.at[step], {"head": peer}))
+        go(remote(kzs.at[take], kzr.at[step], zs.at[step], zr.at[step], {"head": peer}))
     for p in range(pairs // 2, pairs):
         query(p)
-    out = pltpu.make_async_copy(qg, qg_out, local.at[6])
-    out.start()
     value = kz[pl.ds(pl.multiple_of(head * part, part), part), :]
     for step in range(1, shares):
         remote(kzr.at[step], kzr.at[step], zs.at[step], zr.at[step], {"head": head}).wait_recv()
-        value = value + kzr[step]
+        value = value + kzr[step].astype(jnp.float32)
     kg_out[...] = value
     for copy in sent:
         copy.wait_send()
-    out.wait()
 
 
 def per_device(
@@ -387,12 +395,13 @@
     return pl.pallas_call(
         functools.partial(kernel, groups, shares),
         out_shape=(
-            jax.ShapeDtypeStruct((rows, idx_heads, dim), f32),
-            jax.ShapeDtypeStruct((rows // shares, dim), f32),
+            vmem((rows, idx_heads, dim), f32),
+            vmem((rows // shares, dim), f32),
         ),
-        in_specs=[pl.BlockSpec(memory_space=pltpu.SMEM)] + [pl.BlockSpec(memory_space=pl.ANY)] * 6,
-        out_specs=(pl.BlockSpec(memory_space=pl.ANY), pl.BlockSpec(memory_space=pltpu.VMEM)),
+        in_specs=[pl.BlockSpec(memory_space=pl.ANY)] * 7,
+        out_specs=(pl.BlockSpec(memory_space=pltpu.VMEM),) * 2,
         scratch_shapes=[
+            pltpu.SMEM(block_order.shape, block_order.dtype),
             vmem((cycle, latent, rows), bf16),
             vmem((cycle, rows, dim), bf16),
             vmem((heads, latent, rows), bf16),
@@ -413,8 +422,8 @@
             vmem((groups, 2, rows, dim), bf16),
             vmem((2, rows, dim), f32),
             vmem((rows, dim), f32),
-            vmem((shares, rows // shares, dim), f32),
-            vmem((rows, idx_heads, dim), f32),
+            vmem((rows, dim), bf16),
+            vmem((shares, rows // shares, dim), bf16),
             dma((7,)),
             dma((2, groups)), dma((2, groups)), dma((2, groups)), dma((2, groups)),
             dma((2, groups + 1, shares)), dma((2, groups + 1, shares)),

time: 46.3 us -> 40.2 us (0.87)
  Pallas kernels: 41.8 us -> 37.9 us
  local copies, waits for them, and re-layouts: 3.59 us -> 1.58 us
    pallas_call x1, Pallas kernels: 41.8 us -> 37.9 us  [per_device(): pl.pallas_call(functools.partial(kernel, groups, shares), out_shape=(vmem...]
    unnamed x2, local copies, waits for them, and re-layouts: 3.59 us -> 1.58 us
where the time goes in v2:
time: 40.2 us; the launch traced here: 40.1 us
  Pallas kernels  37.9 us (94%)
  local copies, waits for them, and re-layouts  1.58 us (4%)
  between operations  0.64 us (2%)
    pallas_call x1, Pallas kernels, per_device(): pl.pallas_call(functools.partial(kernel, groups, shares), out_shape=(vmem...  37.9 us
    unnamed x2, local copies, waits for them, and re-layouts  1.58 us

profile of v2, /device:TPU:0, one launch (start us, length us, event | category | flops | bytes accessed | tf_op | source)
XLA Modules:
  0.0 40.1 jit_solution(9818108283720120142)
XLA Ops:
  0.6 37.9 %indexer.1 = (f32[128,16,128]{2,1,0:T(8,128)S(1)}, f32[32,128]{1,0:T(8,128)S(1)}) custom-call(s32[16]{0:T(128)} %order_far.1, bf16[576,128]{1,0:T(8,128)(2,1)} %bitcast.5, bf16[128,128]{1,0:T(8,128)(2,1)} %idx.1, bf16[128,16,128]{2,1,0:T(8,128)(2,1)} %iq.1, bf16[16,128]{1,0:T(8,128)(2,1)} %bitcast.7, bf16[32,576,128]{2,1,0:T(8,128)(2,1)} %bitcast.4, ...), custom_call_target="tpu_custom_call" | custom-call | tf_op jit(solution)/shard_map/indexer/pallas_call | solution.py:395
  38.5 1.0 %copy.11 = f32[128,16,128]{2,1,0:T(8,128)} copy(f32[128,16,128]{2,1,0:T(8,128)S(1)} %get-tuple-element.2) | data formatting | bytes 2097152
  39.5 0.6 %copy.12 = f32[32,128]{1,0:T(8,128)} copy(f32[32,128]{1,0:T(8,128)S(1)} %get-tuple-element.3) | data formatting | bytes 32768

commit v3 on v2

--- a/solution.py
+++ b/solution.py
@@ -64,7 +64,7 @@
             pl.semaphore_signal(barrier, 1, device_id={"ctx": peer + j}, device_id_type=MESH)
     pl.semaphore_signal(barrier, 1, device_id={"ctx": sibling}, device_id_type=MESH)
     for step in range(1, shares):
-        peer = lax.rem(head + step, shares)
+        peer = partner(head, step, shares)
         pl.semaphore_signal(barrier, 1, device_id={"head": peer}, device_id_type=MESH)
     for copy in own:
         copy.start()
@@ -76,11 +76,23 @@
         copy.start()
         sent.append(copy)
 
-    for k, (src, dst) in enumerate(((idx, all_idx), (lat, all_lat))):
-        go(remote(src, dst.at[ctx], fs.at[k, 0], fr.at[k, 0], {"ctx": sibling}))
-        for step in range(1, groups):
+    def spread(k, step):
+        src, dst = ((idx, all_idx), (lat, all_lat))[k]
+        if step:
             peer = partner(group, step, groups) * 2 + core
             go(remote(src, dst.at[ctx], ds.at[k, step], dr.at[k, step], {"ctx": peer}))
+        else:
+            go(remote(src, dst.at[ctx], fs.at[k, 0], fr.at[k, 0], {"ctx": sibling}))
+
+    near = min(3, groups)
+    for k in range(2):
+        spread(k, 0)
+    for k in range(2):
+        for step in range(1, near):
+            spread(k, step)
+    for step in range(near, groups):
+        for k in range(2):
+            spread(k, step)
 
     def relay(k, step):
         source = partner(group, step, groups) * 2 + core
@@ -146,8 +158,8 @@
 
     def exchange(k, slot, width):
         send, recv = ((lsend, lrecv), (tsend, trecv))[k]
-        for step in range(1, shares):
-            peer = lax.rem(head + step, shares)
+        for step in range(shares - 1, 0, -1):
+            peer = partner(head, step, shares)
             go(
                 remote(
                     send.at[peer, slot, :, pl.ds(0, width)],
@@ -197,13 +209,9 @@
             total = total + jnp.exp2(scores[:, rows:] - shift[1:])
         return total
 
-    def score(step):
+    def score(step, split):
         source = partner(group, step, groups)
-        if step < groups - 1:
-            arrive(1, step)
-            keys[...] = jnp.concatenate((all_lat[2 * source], all_lat[2 * source + 1]), axis=1).T
-            total = attend(keys)
-        else:
+        if split:
             parts = []
             for k, device in enumerate((2 * source + core, 2 * source + 1 - core)):
                 if k:
@@ -211,10 +219,13 @@
                 half_keys = keys.at[pl.ds(k * rows, rows)]
                 half_keys[...] = all_lat[device].T
                 parts.append(attend(half_keys))
-            near, other = parts
             total = jnp.concatenate(
-                (jnp.where(core == 0, near, other), jnp.where(core == 0, other, near)), axis=0
-            )
+                (jnp.where(core == 0, *parts), jnp.where(core == 0, *parts[::-1])), axis=0
+            )
+        else:
+            arrive(1, step)
+            keys[...] = jnp.concatenate((all_lat[2 * source], all_lat[2 * source + 1]), axis=1).T
+            total = attend(keys)
         packed, low = pack(total, source)
         deal(1, step, packed)
         if step == 0:
@@ -227,20 +238,24 @@
     own[2].wait()
     arrive(0, 0)
     logits(0)
+    for step in range(1, near):
+        relay(0, step)
     for copy in own[3:6]:
         copy.wait()
-    score(0)
-    for step in range(1, groups):
-        relay(0, step)
-    for step in range(1, groups):
+    score(0, False)
+    for step in range(1, near):
         arrive(0, step)
         logits(step)
-    for step in range(1, min(3, groups)):
+    for step in range(1, near):
         relay(1, step)
     for step in range(1, groups):
-        score(step)
-        if step + 2 < groups:
-            relay(1, step + 2)
+        if near <= step + 1 < groups:
+            relay(0, step + 1)
+        if step >= near:
+            arrive(0, step)
+            logits(step)
+            relay(1, step)
+        score(step, step != near - 1)
 
     shape = (share, 2 * rows)
     token = head * share + lax.broadcasted_iota(jnp.int32, shape, 0)
@@ -305,14 +320,14 @@
         if seen is not None:
             value = jnp.where(seen, value, 0.0)
         gall[head, slot, :, :width] = value.astype(jnp.bfloat16)
-        for step in range(1, shares):
-            peer = lax.rem(head + step, shares)
+        for step in range(shares - 1, 0, -1):
+            peer = partner(head, step, shares)
             piece = gall.at[head, slot, :, pl.ds(0, width)]
             go(remote(piece, piece, gs.at[slot, step], gr.at[slot, step], {"head": peer}))
 
     def granted(slot):
         for step in range(1, shares):
-            source = lax.rem(head + shares - step, shares)
+            source = partner(head, step, shares)
             piece = gall.at[source, slot, :, pl.ds(0, table[slot][2])]
             remote(piece, piece, gs.at[slot, step], gr.at[slot, step], {"head": source}).wait_recv()
 
@@ -323,12 +338,14 @@
         source = partner(group, slot, groups)
         rate[...] = unpack(slot, source)
         span = slice(slot * 2 * rows, (slot + 1) * 2 * rows)
-        for h in range(idx_heads):
-            cols = slice(h * rows, (h + 1) * rows)
-            coefs[span, cols] = (rate[...] * weights[h : h + 1]).astype(jnp.bfloat16) * coefs[
-                span, cols
-            ]
-        total = jnp.dot(coefs[span, :], iqf[...], preferred_element_type=jnp.float32)
+        total = jnp.zeros((2 * rows, dim), jnp.float32)
+        for p in range(idx_heads // 2):
+            cols = slice(2 * p * rows, 2 * (p + 1) * rows)
+            value = jnp.concatenate(
+                [rate[...] * weights[h : h + 1] for h in (2 * p, 2 * p + 1)], axis=1
+            ).astype(jnp.bfloat16) * coefs[span, cols]
+            coefs[span, cols] = value
+            total = total + jnp.dot(value, iqf[cols, :], preferred_element_type=jnp.float32)
         if slot == 0:
             kown[...] = total.reshape(2, rows, dim)
         ksend[slot] = total.astype(jnp.bfloat16).reshape(2, rows, dim)
@@ -366,8 +383,8 @@
     kz[...] = value
     kzs[...] = value.astype(jnp.bfloat16)
     part = rows // shares
-    for step in range(1, shares):
-        peer = lax.rem(head + step, shares)
+    for step in range(shares - 1, 0, -1):
+        peer = partner(head, step, shares)
         take = pl.ds(pl.multiple_of(peer * part, part), part)
         go(remote(kzs.at[take], kzr.at[step], zs.at[step], zr.at[step], {"head": peer}))
     for p in range(pairs // 2, pairs):
@@ -381,6 +398,16 @@
         copy.wait_send()
 
 
+def store(qg, kg, qg_out, kg_out, sems):
+    copies = [
+        pltpu.make_async_copy(qg, qg_out, sems.at[0]), pltpu.make_async_copy(kg, kg_out, sems.at[1])
+    ]
+    for copy in copies:
+        copy.start()
+    for copy in copies:
+        copy.wait()
+
+
 def per_device(
     block_order, query_latent, key_latent, normalizer, indexer_query, indexer_key, indexer_weight
 ):
@@ -392,7 +419,7 @@
     share = rows // 2 // shares
     bf16, f32 = jnp.bfloat16, jnp.float32
     dma, vmem = pltpu.SemaphoreType.DMA, pltpu.VMEM
-    return pl.pallas_call(
+    results = pl.pallas_call(
         functools.partial(kernel, groups, shares),
         out_shape=(
             vmem((rows, idx_heads, dim), f32),
@@ -437,6 +464,18 @@
         block_order, key_latent.T, indexer_key, indexer_query, indexer_weight.T,
         query_latent.transpose(1, 2, 0), normalizer.T,
     )
+    results = [pltpu.with_memory_space_constraint(x, pltpu.VMEM) for x in results]
+    return pl.pallas_call(
+        store,
+        out_shape=(
+            jax.ShapeDtypeStruct((rows, idx_heads, dim), f32),
+            jax.ShapeDtypeStruct((rows // shares, dim), f32),
+        ),
+        in_specs=[pl.BlockSpec(memory_space=pltpu.VMEM)] * 2,
+        out_specs=(pl.BlockSpec(memory_space=pl.ANY),) * 2,
+        scratch_shapes=[dma((2,))],
+        name="store",
+    )(*results)
 
 
 def solution(mesh):

time: 40.2 us -> 39.1 us (0.973)
  local copies, waits for them, and re-layouts: 1.58 us -> 0 us
    unnamed x2 -> x0, local copies, waits for them, and re-layouts: 1.58 us -> none
    pallas_call x0 -> x1, Pallas kernels: none -> 0.99 us  [per_device(): pl.pallas_call(store, out_shape=(jax.ShapeDtypeStruct((rows, idx_heads, d...]
    pallas_call x1, Pallas kernels: 37.9 us -> 37.3 us  [per_device(): pl.pallas_call(functools.partial(kernel, groups, shares), out_shape=(vmem...]
where the time goes in v3:
time: 39.1 us; the launch traced here: 39 us
  Pallas kernels  38.3 us (98%)
  between operations  0.64 us (2%)
    pallas_call x1, Pallas kernels, per_device(): pl.pallas_call(functools.partial(kernel, groups, shares), out_shape=(vmem...  37.3 us
    pallas_call x1, Pallas kernels, per_device(): pl.pallas_call(store, out_shape=(jax.ShapeDtypeStruct((rows, idx_heads, d...  0.99 us

profile of v3, /device:TPU:0, one launch (start us, length us, event | category | flops | bytes accessed | tf_op | source)
XLA Modules:
  0.0 39.0 jit_solution(8366423559811401347)
XLA Ops:
  0.6 37.3 %indexer.1 = (f32[128,16,128]{2,1,0:T(8,128)S(1)}, f32[32,128]{1,0:T(8,128)S(1)}) custom-call(s32[16]{0:T(128)} %order_far.1, bf16[576,128]{1,0:T(8,128)(2,1)} %bitcast.5, bf16[128,128]{1,0:T(8,128)(2,1)} %idx.1, bf16[128,16,128]{2,1,0:T(8,128)(2,1)} %iq.1, bf16[16,128]{1,0:T(8,128)(2,1)} %bitcast.7, bf16[32,576,128]{2,1,0:T(8,128)(2,1)} %bitcast.4, ...), custom_call_target="tpu_custom_call" | custom-call | tf_op jit(solution)/shard_map/indexer/pallas_call | solution.py:422
  38.0 1.0 %store.1 = (f32[128,16,128]{2,1,0:T(8,128)}, f32[32,128]{1,0:T(8,128)}) custom-call(f32[128,16,128]{2,1,0:T(8,128)S(1)} %get-tuple-element.4.qg, f32[32,128]{1,0:T(8,128)S(1)} %get-tuple-element.5.kg), custom_call_target="tpu_custom_call" | custom-call | tf_op jit(solution)/shard_map/store/pallas_call | solution.py:468
